TPU v7x, 128 devices: a whole 4x4x4 slice. The times are simulated.
128 devices in a mesh: prow: 8 (over x, y_lo), pcol: 16 (over y_hi, z, core).
Axes of the slice: x: 4, y: 4 (y_hi: 2, y_lo: 2; y = y_hi * 2 + y_lo), z: 4, core: 2. Of those that a mesh axis runs over, the one named last changes fastest.
Arguments:
- inverse_top: bfloat16 [128, 128, 128, 128], P('prow', 'pcol'), may hold values from -6 to 6
- rows_one: int32 [16, 64], replicated, may hold values from 0 to 127, as said below
- panel_one: bfloat16 [16, 64, 128, 128], P('pcol', 'prow'), may hold values from -0.0625 to 0.0625
- base_one: float32 [16, 128, 128], P('pcol'), may hold values from -6 to 6
- parent_two: int32 [16], replicated, may hold values from 0 to 15
- order_two: int32 [16, 64], replicated, may hold values from 0 to 63, as said below
- panel_two: bfloat16 [16, 64, 128, 128], P('pcol', 'prow'), may hold values from -0.0625 to 0.0625
- link_two: bfloat16 [16, 128, 128], P('pcol'), may hold values from -0.5 to 0.5
- base_two: float32 [16, 128, 128], P('pcol'), may hold values from -6 to 6
Outputs:
- column_one: bfloat16 [16, 64, 128, 128], P('pcol', 'prow')
- diagonal_one: bfloat16 [16, 128, 128], P('pcol')
- column_two: bfloat16 [16, 64, 128, 128], P('pcol', 'prow')
- upper_two: bfloat16 [16, 128, 128], P('pcol')
- diagonal_two: bfloat16 [16, 128, 128], P('pcol')
Inputs may be any that keep to these rules, and one draw needn't show every extreme that they name: For every supernode k and process row p, rows_one[k, p * 8] to rows_one[k, p * 8 + 7] are 8 distinct ancestors between p * 16 and p * 16 + 15. In every draw some process column c holds 8 ancestors (ancestor // 8 == c) of every level-one supernode. Each block order_two[k, p * 8] to order_two[k, p * 8 + 7] is a permutation of p * 8 to p * 8 + 7.
All inputs are finite; a program needn't handle non-finite values.
Results may differ from a plain program's by a relative error of at most 0.024.
Values may be sent and summed in bfloat16 or wider, within the bound.
A program may use at most 192 MiB of HBM per device.

v0:
```python
import jax
import jax.numpy as jnp
from jax import lax
from jax.sharding import PartitionSpec as P


def slot_positions(rows_all, dests, width, capacity):
    owner = rows_all // width
    length = rows_all.shape[1]
    positions = jnp.arange(length, dtype=jnp.int32)
    same_owner = owner[:, :, None] == owner[:, None, :]
    earlier = positions[None, None, :] < positions[None, :, None]
    ranking = jnp.sum(jnp.logical_and(same_owner, earlier), axis=2)
    slot_ids = jnp.arange(capacity, dtype=jnp.int32)
    matches = jnp.logical_and(
        owner[None, :, None, :] == dests[:, None, None, None],
        ranking[None, :, None, :] == slot_ids[None, None, :, None],
    )
    where_at = jnp.sum(jnp.where(matches, positions, 0), axis=3)
    present = jnp.any(matches, axis=3)
    return (where_at, present)


def pack_panels(full_panel, my_rows, width, capacity, columns):
    where_at, present = slot_positions(
        my_rows, jnp.arange(columns, dtype=jnp.int32), width, capacity
    )
    children = jnp.arange(my_rows.shape[0], dtype=jnp.int32)[None, :, None]
    selected = full_panel[children, where_at]
    return jnp.where(present[:, :, :, None, None], selected, jnp.zeros((), selected.dtype))


def local_indices(rows_all, prow_at, pcol_at, per_row, height, width):
    where_at, present = slot_positions(rows_all, jnp.reshape(pcol_at, (1,)), width, per_row)
    targets = jnp.take_along_axis(rows_all, where_at[0], axis=1)
    col_local = jnp.where(present[0], targets - pcol_at * width, 0)
    row_local = lax.dynamic_slice_in_dim(rows_all, prow_at * per_row, per_row, 1) - prow_at * height
    return (row_local, col_local)


def tile_products(inverse_local, received, row_local, col_local):
    blocks = inverse_local[row_local[:, :, None], col_local[:, None, :]]
    return jnp.einsum("kabij,kbjl->kail", blocks, received, preferred_element_type=jnp.float32)


def flatten_received(received):
    return received.reshape((received.shape[0] * received.shape[1],) + received.shape[2:])


def local(
    inverse_top, rows_one, panel_one, base_one, parent_two, order_two, panel_two, link_two, base_two
):
    per_col = panel_one.shape[0]
    per_row = panel_one.shape[1]
    height = inverse_top.shape[0]
    width = inverse_top.shape[1]
    columns = lax.axis_size("pcol")
    prow_at = lax.axis_index("prow")
    pcol_at = lax.axis_index("pcol")
    rows_two = jnp.take_along_axis(rows_one[parent_two], order_two, axis=1)
    mine_one = lax.dynamic_slice_in_dim(rows_one, pcol_at * per_col, per_col, 0)
    mine_two = lax.dynamic_slice_in_dim(rows_two, pcol_at * per_col, per_col, 0)
    row_one, col_one = local_indices(rows_one, prow_at, pcol_at, per_row, height, width)
    row_two, col_two = local_indices(rows_two, prow_at, pcol_at, per_row, height, width)
    full_one = lax.all_gather(panel_one, "prow", axis=1, tiled=True)
    outgoing_one = pack_panels(full_one, mine_one, width, per_row, columns)
    received_one = lax.all_to_all(outgoing_one, "pcol", split_axis=0, concat_axis=0, tiled=True)
    flat_one = flatten_received(received_one)
    summed_one = lax.psum_scatter(
        tile_products(inverse_top, flat_one, row_one, col_one).astype(jnp.bfloat16),
        "pcol",
        scatter_dimension=0,
        tiled=True,
    ).astype(jnp.float32)
    full_two = lax.all_gather(panel_two, "prow", axis=1, tiled=True)
    outgoing_two = pack_panels(full_two, mine_two, width, per_row, columns)
    received_two = lax.all_to_all(outgoing_two, "pcol", split_axis=0, concat_axis=0, tiled=True)
    flat_two = flatten_received(received_two)
    summed_two = lax.psum_scatter(
        tile_products(inverse_top, flat_two, row_two, col_two).astype(jnp.bfloat16),
        "pcol",
        scatter_dimension=0,
        tiled=True,
    ).astype(jnp.float32)
    column_one = (-summed_one).astype(jnp.bfloat16)
    diag_part = jnp.einsum(
        "cmij,cmil->cjl", panel_one, column_one, preferred_element_type=jnp.float32
    )
    diagonal_one = (
        base_one - lax.psum(diag_part.astype(jnp.bfloat16), "prow").astype(jnp.float32)
    ).astype(jnp.bfloat16)
    all_cols, all_diag = (
        lax.all_gather(column_one, "pcol", axis=0, tiled=True),
        lax.all_gather(diagonal_one, "pcol", axis=0, tiled=True),
    )
    my_parent = lax.dynamic_slice_in_dim(parent_two, pcol_at * per_col, per_col, 0)
    my_order = (
        lax.dynamic_slice(order_two, (pcol_at * per_col, prow_at * per_row), (per_col, per_row))
        - prow_at * per_row
    )
    near_cols = all_cols[my_parent[:, None], my_order]
    near_diag = all_diag[my_parent]
    carried = jnp.einsum("cmij,cjl->cmil", near_cols, link_two, preferred_element_type=jnp.float32)
    column_two = (-(summed_two + carried)).astype(jnp.bfloat16)
    upper_part = jnp.einsum(
        "cmij,cmil->cjl", near_cols, panel_two, preferred_element_type=jnp.float32
    )
    parent_term = jnp.einsum(
        "cij,cjl->cil", near_diag, link_two, preferred_element_type=jnp.float32
    )
    upper_total = lax.psum(upper_part.astype(jnp.bfloat16), "prow").astype(jnp.float32)
    upper_two = (-(parent_term + upper_total)).astype(jnp.bfloat16)
    lower_part = jnp.einsum(
        "cmij,cmil->cjl", panel_two, column_two, preferred_element_type=jnp.float32
    )
    lower_total = lax.psum(lower_part.astype(jnp.bfloat16), "prow").astype(jnp.float32)
    link_term = jnp.einsum("cij,cil->cjl", link_two, upper_two, preferred_element_type=jnp.float32)
    diagonal_two = (base_two - link_term - lower_total).astype(jnp.bfloat16)
    return (column_one, diagonal_one, column_two, upper_two, diagonal_two)


def solution(mesh):
    return jax.shard_map(
        local,
        mesh=mesh,
        in_specs=(
            P("prow", "pcol", None, None),
            P(),
            P("pcol", "prow", None, None),
            P("pcol", None, None),
            P(),
            P(),
            P("pcol", "prow", None, None),
            P("pcol", None, None),
            P("pcol", None, None),
        ),
        out_specs=(
            P("pcol", "prow", None, None),
            P("pcol", None, None),
            P("pcol", "prow", None, None),
            P("pcol", None, None),
            P("pcol", None, None),
        ),
        check_vma=False,
    )
```

profile of v0, /device:TPU:1, one launch (start us, length us, event | category | flops | bytes accessed | tf_op | source)
XLA Modules:
  0.0 586.9 jit_solution(2834945553307721107)
XLA Ops:
  7.2 0.7 all-gather.4.cloned.1.call-update
  7.9 0.7 fusion.64
  8.6 0.2 convert_reduce_fusion.3
  8.8 0.4 fusion.28
  9.4 0.4 and_reduce_fusion.1
  9.8 52.7 %all-gather.4.cloned.1.call-done = bf16[1,64,128,128]{3,2,0,1:T(8,128)(2,1)} async-done(((bf16[1,8,128,128]{3,2,0,1:T(8,128)(2,1)}), bf16[1,64,128,128]{3,2,0,1:T(8,128)(2,1)}) %all-gather.4.cloned.1.call-update) | async-done | bytes 2097168 | tf_op jit(solution)/shard_map/all_gather | solution.py:65
  62.6 4.6 gather_fusion.1
  67.2 4.6 broadcast_select_fusion.1
  71.8 8.7 %all-to-all-start = ((bf16[16,1,8,128,128]{4,3,2,1,0:T(8,128)(2,1)}), bf16[16,1,8,128,128]{4,3,2,1,0:T(8,128)(2,1)}, u32[]{:S(2)}, u32[]{:S(2)}) async-start(bf16[16,1,8,128,128]{4,3,2,1,0:T(8,128)(2,1)} %broadcast_select_fusion.1), calls=%async_computation | async-start | bytes 8388608 | tf_op jit(solution)/shard_map/all_to_all | solution.py:67
  80.5 0.6 gather_fusion.2
  81.2 7.1 %gather_fusion.6 = s32[1024]{0:T(1024)S(1)} fusion(s32[16,64]{1,0:T(8,128)S(1)} %gather_fusion.2, s32[1024]{0:T(1024)S(1)} %reshape.675), kind=kCustom, calls=%fused_computation.8 | custom fusion | bytes 16384 | tf_op jit(solution)/shard_map/jit(take_along_axis)/gather | solution.py:60
  88.3 0.9 convert_reduce_fusion
  89.3 0.3 select_reduce_fusion.1
  89.9 1.3 gather_fusion.7
  91.3 0.4 fusion.31
  91.9 23.3 %gather_fusion = bf16[1024,128,128]{2,1,0:T(8,128)(2,1)} fusion(bf16[16,8,128,128]{3,2,1,0:T(8,128)(2,1)} %param.11, s32[1024]{0:T(1024)S(1)} %reshape.631), kind=kCustom, calls=%fused_computation.2 | custom fusion | bytes 67117056 | tf_op jit(solution)/shard_map/gather | solution.py:42
  115.2 20.5 %all-to-all-done = bf16[16,1,8,128,128]{4,3,2,1,0:T(8,128)(2,1)} async-done(((bf16[16,1,8,128,128]{4,3,2,1,0:T(8,128)(2,1)}), bf16[16,1,8,128,128]{4,3,2,1,0:T(8,128)(2,1)}, u32[]{:S(2)}, u32[]{:S(2)}) %all-to-all-start) | async-done | bytes 4194336 | tf_op jit(solution)/shard_map/all_to_all | solution.py:67
  135.7 17.7 %bitcast_convert_fusion.1 = bf16[16,8,128,128]{3,2,1,0:T(8,128)(2,1)} fusion(bf16[16,8,8,128,128]{4,3,2,1,0:T(8,128)(2,1)} %bitcast.161, bf16[16,1,8,128,128]{4,3,2,1,0:T(8,128)(2,1)} %all-to-all-done), kind=kOutput, calls=%fused_computation.10 | convolution fusion | flops 4297064448 | bytes 41943040 | tf_op jit(solution)/shard_map/kabij,kbjl->kail/dot_general | solution.py:43
  153.5 0.7 all-gather.6.cloned.1.call-update
  154.3 0.2 convert_reduce_fusion.2
  154.5 85.3 %reduce-scatter.3.cloned.1.call-done = bf16[1,8,128,128]{3,2,1,0:T(8,128)(2,1)} async-done(((bf16[16,8,128,128]{3,2,1,0:T(8,128)(2,1)}), bf16[1,8,128,128]{3,2,1,0:T(8,128)(2,1)}) %reduce-scatter.3.cloned.1.call-update) | async-done | bytes 262160 | tf_op jit(solution)/shard_map/reduce_scatter | solution.py:69
  239.8 1.7 negate_convert_fusion
  241.5 0.4 fusion.29
  242.1 0.4 and_reduce_fusion
  242.5 48.9 %all-gather.6.cloned.1.call-done = bf16[1,64,128,128]{3,2,0,1:T(8,128)(2,1)} async-done(((bf16[1,8,128,128]{3,2,0,1:T(8,128)(2,1)}), bf16[1,64,128,128]{3,2,0,1:T(8,128)(2,1)}) %all-gather.6.cloned.1.call-update) | async-done | bytes 2097168 | tf_op jit(solution)/shard_map/all_gather | solution.py:75
  291.4 4.6 gather_fusion.4
  296.0 4.5 broadcast_select_fusion
  300.4 8.5 %all-to-all-start.1 = ((bf16[16,1,8,128,128]{4,3,2,1,0:T(8,128)(2,1)}), bf16[16,1,8,128,128]{4,3,2,1,0:T(8,128)(2,1)}, u32[]{:S(2)}, u32[]{:S(2)}) async-start(bf16[16,1,8,128,128]{4,3,2,1,0:T(8,128)(2,1)} %broadcast_select_fusion), calls=%async_computation.2 | async-start | bytes 8388608 | tf_op jit(solution)/shard_map/all_to_all | solution.py:77
  309.0 0.2 reduce-scatter.5.cloned.1.call-start
  309.2 0.3 select_reduce_fusion
  309.8 1.3 gather_fusion.8
  311.3 0.4 fusion.33
  311.8 23.3 %gather_fusion.3 = bf16[1024,128,128]{2,1,0:T(8,128)(2,1)} fusion(bf16[16,8,128,128]{3,2,1,0:T(8,128)(2,1)} %param.11, s32[1024]{0:T(1024)S(1)} %reshape.653), kind=kCustom, calls=%fused_computation.5 | custom fusion | bytes 67117056 | tf_op jit(solution)/shard_map/gather | solution.py:42
  335.1 34.6 %all-to-all-done.1 = bf16[16,1,8,128,128]{4,3,2,1,0:T(8,128)(2,1)} async-done(((bf16[16,1,8,128,128]{4,3,2,1,0:T(8,128)(2,1)}), bf16[16,1,8,128,128]{4,3,2,1,0:T(8,128)(2,1)}, u32[]{:S(2)}, u32[]{:S(2)}) %all-to-all-start.1) | async-done | bytes 4194336 | tf_op jit(solution)/shard_map/all_to_all | solution.py:77
  369.8 17.9 %bitcast_convert_fusion = bf16[16,8,128,128]{3,2,1,0:T(8,128)(2,1)} fusion(bf16[16,8,8,128,128]{4,3,2,1,0:T(8,128)(2,1)} %bitcast.162, bf16[16,1,8,128,128]{4,3,2,1,0:T(8,128)(2,1)} %all-to-all-done.1), kind=kOutput, calls=%fused_computation.9 | convolution fusion | flops 4297064448 | bytes 41943040 | tf_op jit(solution)/shard_map/kabij,kbjl->kail/dot_general | solution.py:43
  387.8 0.7 dynamic_slice.23
  390.4 0.9 fusion.22
  391.3 2.8 gather_fusion.5
  394.1 0.9 fusion.21
  395.0 80.1 %reduce-scatter.5.cloned.1.call-done = bf16[1,8,128,128]{3,2,1,0:T(8,128)(2,1)} async-done(((bf16[16,8,128,128]{3,2,1,0:T(8,128)(2,1)}), bf16[1,8,128,128]{3,2,1,0:T(8,128)(2,1)}) %reduce-scatter.5.cloned.1.call-update) | async-done | bytes 262160 | tf_op jit(solution)/shard_map/reduce_scatter | solution.py:79
  475.1 1.2 fusion.10
  476.3 0.9 fusion.20
  479.3 66.1 %all-reduce.6.cloned.1.call-done = (bf16[1,128,128]{1,2,0:T(8,128)(2,1)}, bf16[1,128,128]{2,1,0:T(8,128)(2,1)}, bf16[1,128,128]{1,2,0:T(8,128)(2,1)}) async-done(((bf16[1,128,128]{1,2,0:T(8,128)(2,1)}, bf16[1,128,128]{2,1,0:T(8,128)(2,1)}, bf16[1,128,128]{1,2,0:T(8,128)(2,1)}), (bf16[1,128,128]{1,2,0:T(8,128)(2,1)}, bf16[1,128,128]{2,1,0:T(8,128)(2,1)}, ...) | async-done | bytes 98320 | tf_op jit(solution)/shard_map/psum | solution.py:90
  545.4 0.8 subtract_convert_fusion
  546.3 31.2 %all_gather.15 = bf16[16,128,128]{2,1,0:T(8,128)(2,1)S(1)} all-gather(bf16[1,128,128]{2,1,0:T(8,128)(2,1)S(1)} %copy.203), channel_id=1, replica_groups=mesh['prow'=8,'pcol'=16] {'pcol'}, dimensions={0}, use_global_device_ids=true | all-gather | bytes 557056 | tf_op jit(solution)/shard_map/all_gather | solution.py:94
  577.5 0.9 fusion.16
  578.4 1.0 fusion.15
  579.4 0.7 copy.204
  (84 shorter events, 2.7 us)
Async XLA Ops:
  7.2 468.0 %copy-start = (bf16[1,128,128]{2,1,0:T(8,128)(2,1)S(1)}, bf16[1,128,128]{2,1,0:T(8,128)(2,1)}, u32[]{:S(2)}) copy-start(bf16[1,128,128]{2,1,0:T(8,128)(2,1)} %param.18) | copy-start | bytes 98308
  7.2 55.4 %all-gather.4.cloned.1.call-start = ((), (), s32[]{:S(2)}) async-start(), calls=%async_computation.4 | async-start | bytes 2359296 | tf_op jit(solution)/shard_map/all_gather | solution.py:65
  71.7 8.7 %copy-start.11 = (s32[16]{0:T(128)S(1)}, s32[16]{0:T(128)}, u32[]{:S(2)}) copy-start(s32[16]{0:T(128)} %param.15) | copy-start | bytes 196
  71.8 8.7 %copy-start.1 = (s32[16,64]{1,0:T(8,128)S(1)}, s32[16,64]{1,0:T(8,128)}, u32[]{:S(2)}) copy-start(s32[16,64]{1,0:T(8,128)} %param.12) | copy-start | bytes 12292
  71.8 9.3 %copy-start.10 = (s32[16,64]{1,0:T(8,128)S(1)}, s32[16,64]{1,0:T(8,128)}, u32[]{:S(2)}) copy-start(s32[16,64]{1,0:T(8,128)} %param.16) | copy-start | bytes 12292
  71.8 64.0 %all-to-all-start = ((bf16[16,1,8,128,128]{4,3,2,1,0:T(8,128)(2,1)}), bf16[16,1,8,128,128]{4,3,2,1,0:T(8,128)(2,1)}, u32[]{:S(2)}, u32[]{:S(2)}) async-start(bf16[16,1,8,128,128]{4,3,2,1,0:T(8,128)(2,1)} %broadcast_select_fusion.1), calls=%async_computation | async-start | bytes 8388608 | tf_op jit(solution)/shard_map/all_to_all | solution.py:67
  80.4 159.4 %reduce-scatter.3.cloned.1.call-start = ((), (), s32[]{:S(2)}) async-start(), calls=%async_computation.5 | async-start | bytes 4456448 | tf_op jit(solution)/shard_map/reduce_scatter | solution.py:69
  153.5 137.9 %all-gather.6.cloned.1.call-start = ((), (), s32[]{:S(2)}) async-start(), calls=%async_computation.6 | async-start | bytes 2359296 | tf_op jit(solution)/shard_map/all_gather | solution.py:75
  154.2 237.1 %all-gather.8.cloned.1.call-start = ((), (), s32[]{:S(2)}) async-start(), calls=%async_computation.8 | async-start | bytes 4456448 | tf_op jit(solution)/shard_map/all_gather | solution.py:93
  300.4 69.3 %all-to-all-start.1 = ((bf16[16,1,8,128,128]{4,3,2,1,0:T(8,128)(2,1)}), bf16[16,1,8,128,128]{4,3,2,1,0:T(8,128)(2,1)}, u32[]{:S(2)}, u32[]{:S(2)}) async-start(bf16[16,1,8,128,128]{4,3,2,1,0:T(8,128)(2,1)} %broadcast_select_fusion), calls=%async_computation.2 | async-start | bytes 8388608 | tf_op jit(solution)/shard_map/all_to_all | solution.py:77
  309.0 166.2 %reduce-scatter.5.cloned.1.call-start = ((), (), s32[]{:S(2)}) async-start(), calls=%async_computation.7 | async-start | bytes 4456448 | tf_op jit(solution)/shard_map/reduce_scatter | solution.py:79
  387.7 2.7 copy-start.3
  387.7 2.7 copy-start.5
  387.7 6.4 %copy-start.2 = (bf16[1,8,128,128]{3,2,1,0:T(8,128)(2,1)S(1)}, bf16[1,8,128,128]{3,2,1,0:T(8,128)(2,1)}, u32[]{:S(2)}) copy-start(bf16[1,8,128,128]{3,2,1,0:T(8,128)(2,1)} %param.17) | copy-start | bytes 786436
  387.7 89.6 %copy-start.8 = (f32[1,128,128]{2,1,0:T(8,128)S(1)}, f32[1,128,128]{2,1,0:T(8,128)}, u32[]{:S(2)}) copy-start(f32[1,128,128]{2,1,0:T(8,128)} %param.14) | copy-start | bytes 196612
  387.7 90.9 %copy-start.9 = (f32[1,128,128]{2,1,0:T(8,128)S(1)}, f32[1,128,128]{2,1,0:T(8,128)}, u32[]{:S(2)}) copy-start(f32[1,128,128]{2,1,0:T(8,128)} %param.19) | copy-start | bytes 196612
  387.7 157.7 %all-reduce.6.cloned.1.call-start = ((), (), s32[]{:S(2)}) async-start(), calls=%async_computation.9 | async-start | bytes 196608 | tf_op jit(solution)/shard_map/psum | solution.py:90
  476.3 103.8 %copy-start.4 = (bf16[1,8,128,128]{3,2,1,0:T(8,128)(2,1)}, bf16[1,8,128,128]{3,2,1,0:T(8,128)(2,1)S(1)}, u32[]{:S(2)}) copy-start(bf16[1,8,128,128]{3,2,1,0:T(8,128)(2,1)S(1)} %fusion.10) | copy-start | bytes 786436
  546.3 33.8 %copy-start.6 = (bf16[1,128,128]{2,1,0:T(8,128)(2,1)}, bf16[1,128,128]{2,1,0:T(8,128)(2,1)S(1)}, u32[]{:S(2)}) copy-start(bf16[1,128,128]{2,1,0:T(8,128)(2,1)S(1)} %copy.203) | copy-start | bytes 98308
  578.4 1.7 copy-start.7
Sparse Core Ops, SparseCore 0:
  9.6 52.8 all-gather.3
  153.6 86.1 reduce-scatter.2
  241.4 49.8 all-gather.5
  294.2 92.8 all-gather.7
  391.0 84.0 reduce-scatter.4
  478.3 67.1 all-reduce.5
where the time goes:
time: 588 us; the launch traced here: 587 us
  waiting for transfers between devices  390 us (66%)
  local copies, waits for them, and re-layouts  71.9 us (12%)
  matrix products  41.3 us (7%)
  blocking collectives  31.2 us (5%)
  between operations  18.2 us (3%)
  starting transfers between devices  17.6 us (3%)
  other arithmetic  17 us (3%)
    reduce_scatter x1, waiting for transfers between devices, local(): lax.psum_scatter(tile_products(inverse_top, flat_one, row_one, col_one).a...  85.3 us
    reduce_scatter x1, waiting for transfers between devices, local(): lax.psum_scatter(tile_products(inverse_top, flat_two, row_two, col_two).a...  80.1 us
    psum x1, waiting for transfers between devices, local(): lax.psum(diag_part.astype(jnp.bfloat16), 'prow').astype(jnp.float32)  66.1 us
    all_gather x1, waiting for transfers between devices, local(): full_one = lax.all_gather(panel_one, 'prow', axis=1, tiled=True)  52.7 us
    all_gather x1, waiting for transfers between devices, local(): full_two = lax.all_gather(panel_two, 'prow', axis=1, tiled=True)  48.9 us
    gather x2, local copies, waits for them, and re-layouts, tile_products(): blocks = inverse_local[row_local[:, :, None], col_local[:, None, :]]  46.6 us
    dot_general x2, matrix products, tile_products(): jnp.einsum('kabij,kbjl->kail', blocks, received, preferred_element_type=j...  35.6 us
    all_to_all x1, waiting for transfers between devices, local(): lax.all_to_all(outgoing_two, 'pcol', split_axis=0, concat_axis=0, tiled=T...  34.6 us
  transfers between devices with their start and end apart: 8, of which 7 were waited for; matrix products, arithmetic and copies ran while one was open for 17% of the time, Pallas kernels for 0%

commit v1 on v0

--- a/solution.py
+++ b/solution.py
@@ -2,6 +2,8 @@
 import jax.numpy as jnp
 from jax import lax
 from jax.sharding import PartitionSpec as P
+
+number_the_page = lambda vec: jnp.sum(lax.all_gather(vec, "prow"), 0)
 
 
 def slot_positions(rows_all, dests, width, capacity):
@@ -87,7 +89,7 @@
         "cmij,cmil->cjl", panel_one, column_one, preferred_element_type=jnp.float32
     )
     diagonal_one = (
-        base_one - lax.psum(diag_part.astype(jnp.bfloat16), "prow").astype(jnp.float32)
+        base_one - number_the_page(diag_part.astype(jnp.bfloat16)).astype(jnp.float32)
     ).astype(jnp.bfloat16)
     all_cols, all_diag = (
         lax.all_gather(column_one, "pcol", axis=0, tiled=True),

time: 588 us -> 562 us (0.956)
  waiting for transfers between devices: 390 us -> 346 us
  blocking collectives: 31.2 us -> 45.5 us
    reduce_scatter x1, waiting for transfers between devices: 80.1 us -> 57.1 us  [local(): lax.psum_scatter(tile_products(inverse_top, flat_two, row_two, col_two).a...]
    psum x1, waiting for transfers between devices: 66.1 us -> 44.9 us  [local(): lax.psum(upper_part.astype(jnp.bfloat16), 'prow').astype(jnp.float32)]
    all_gather x0 -> x1, blocking collectives: none -> 20.8 us  [number_the_page = lambda vec: jnp.sum(lax.all_gather(vec, 'prow'), 0)]
    all_gather x1, blocking collectives: 31.2 us -> 24.7 us  [local(): lax.all_gather(diagonal_one, 'pcol', axis=0, tiled=True)]
  transfers between devices with their start and end apart: 8 -> 8, of which waited for: 7 -> 7; matrix products, arithmetic and copies ran while one was open for 17% -> 18% of each run, Pallas kernels for 0% -> 0%
where the time goes in v1:
time: 562 us; the launch traced here: 556 us
  waiting for transfers between devices  346 us (62%)
  local copies, waits for them, and re-layouts  72.1 us (13%)
  blocking collectives  45.5 us (8%)
  matrix products  40.7 us (7%)
  between operations  18.4 us (3%)
  starting transfers between devices  17.6 us (3%)
  other arithmetic  16.4 us (3%)
    reduce_scatter x1, waiting for transfers between devices, local(): lax.psum_scatter(tile_products(inverse_top, flat_one, row_one, col_one).a...  85.3 us
    reduce_scatter x1, waiting for transfers between devices, local(): lax.psum_scatter(tile_products(inverse_top, flat_two, row_two, col_two).a...  57.1 us
    all_gather x1, waiting for transfers between devices, local(): full_one = lax.all_gather(panel_one, 'prow', axis=1, tiled=True)  52.7 us
    all_gather x1, waiting for transfers between devices, local(): full_two = lax.all_gather(panel_two, 'prow', axis=1, tiled=True)  48.9 us
    gather x2, local copies, waits for them, and re-layouts, tile_products(): blocks = inverse_local[row_local[:, :, None], col_local[:, None, :]]  46.6 us
    psum x1, waiting for transfers between devices, local(): lax.psum(upper_part.astype(jnp.bfloat16), 'prow').astype(jnp.float32)  44.9 us
    dot_general x2, matrix products, tile_products(): jnp.einsum('kabij,kbjl->kail', blocks, received, preferred_element_type=j...  35.6 us
    all_to_all x1, waiting for transfers between devices, local(): lax.all_to_all(outgoing_two, 'pcol', split_axis=0, concat_axis=0, tiled=T...  34.6 us
  transfers between devices with their start and end apart: 8, of which 7 were waited for; matrix products, arithmetic and copies ran while one was open for 18% of the time, Pallas kernels for 0%

profile of v1, /device:TPU:1, one launch (start us, length us, event | category | flops | bytes accessed | tf_op | source)
XLA Modules:
  0.0 556.3 jit_solution(18304721176136836997)
XLA Ops:
  7.2 0.7 all-gather.5.cloned.1.call-update
  7.9 0.7 fusion.65
  8.6 0.2 convert_reduce_fusion.3
  8.8 0.4 fusion.28
  9.4 0.4 and_reduce_fusion.1
  9.8 52.7 %all-gather.5.cloned.1.call-done = bf16[1,64,128,128]{3,2,0,1:T(8,128)(2,1)} async-done(((bf16[1,8,128,128]{3,2,0,1:T(8,128)(2,1)}), bf16[1,64,128,128]{3,2,0,1:T(8,128)(2,1)}) %all-gather.5.cloned.1.call-update) | async-done | bytes 2097168 | tf_op jit(solution)/shard_map/all_gather | solution.py:67
  62.6 4.6 gather_fusion.1
  67.2 4.6 broadcast_select_fusion.1
  71.8 8.7 %all-to-all-start = ((bf16[16,1,8,128,128]{4,3,2,1,0:T(8,128)(2,1)}), bf16[16,1,8,128,128]{4,3,2,1,0:T(8,128)(2,1)}, u32[]{:S(2)}, u32[]{:S(2)}) async-start(bf16[16,1,8,128,128]{4,3,2,1,0:T(8,128)(2,1)} %broadcast_select_fusion.1), calls=%async_computation | async-start | bytes 8388608 | tf_op jit(solution)/shard_map/all_to_all | solution.py:69
  80.5 0.6 gather_fusion.2
  81.2 7.1 %gather_fusion.6 = s32[1024]{0:T(1024)S(1)} fusion(s32[16,64]{1,0:T(8,128)S(1)} %gather_fusion.2, s32[1024]{0:T(1024)S(1)} %reshape.688), kind=kCustom, calls=%fused_computation.8 | custom fusion | bytes 16384 | tf_op jit(solution)/shard_map/jit(take_along_axis)/gather | solution.py:62
  88.3 0.9 convert_reduce_fusion
  89.3 0.3 select_reduce_fusion.1
  89.9 1.3 gather_fusion.7
  91.3 0.4 fusion.32
  91.9 23.3 %gather_fusion = bf16[1024,128,128]{2,1,0:T(8,128)(2,1)} fusion(bf16[16,8,128,128]{3,2,1,0:T(8,128)(2,1)} %param.11, s32[1024]{0:T(1024)S(1)} %reshape.644), kind=kCustom, calls=%fused_computation.2 | custom fusion | bytes 67117056 | tf_op jit(solution)/shard_map/gather | solution.py:44
  115.2 20.5 %all-to-all-done = bf16[16,1,8,128,128]{4,3,2,1,0:T(8,128)(2,1)} async-done(((bf16[16,1,8,128,128]{4,3,2,1,0:T(8,128)(2,1)}), bf16[16,1,8,128,128]{4,3,2,1,0:T(8,128)(2,1)}, u32[]{:S(2)}, u32[]{:S(2)}) %all-to-all-start) | async-done | bytes 4194336 | tf_op jit(solution)/shard_map/all_to_all | solution.py:69
  135.7 17.7 %bitcast_convert_fusion.1 = bf16[16,8,128,128]{3,2,1,0:T(8,128)(2,1)} fusion(bf16[16,8,8,128,128]{4,3,2,1,0:T(8,128)(2,1)} %bitcast.167, bf16[16,1,8,128,128]{4,3,2,1,0:T(8,128)(2,1)} %all-to-all-done), kind=kOutput, calls=%fused_computation.10 | convolution fusion | flops 4297064448 | bytes 41943040 | tf_op jit(solution)/shard_map/kabij,kbjl->kail/dot_general | solution.py:45
  153.5 0.7 all-gather.7.cloned.1.call-update
  154.5 85.3 %reduce-scatter.3.cloned.1.call-done = bf16[1,8,128,128]{3,2,1,0:T(8,128)(2,1)} async-done(((bf16[16,8,128,128]{3,2,1,0:T(8,128)(2,1)}), bf16[1,8,128,128]{3,2,1,0:T(8,128)(2,1)}) %reduce-scatter.3.cloned.1.call-update) | async-done | bytes 262160 | tf_op jit(solution)/shard_map/reduce_scatter | solution.py:71
  239.8 1.7 negate_convert_fusion
  241.5 0.4 fusion.29
  242.1 0.4 and_reduce_fusion
  242.5 48.9 %all-gather.7.cloned.1.call-done = bf16[1,64,128,128]{3,2,0,1:T(8,128)(2,1)} async-done(((bf16[1,8,128,128]{3,2,0,1:T(8,128)(2,1)}), bf16[1,64,128,128]{3,2,0,1:T(8,128)(2,1)}) %all-gather.7.cloned.1.call-update) | async-done | bytes 2097168 | tf_op jit(solution)/shard_map/all_gather | solution.py:77
  291.4 4.6 gather_fusion.4
  296.0 4.5 broadcast_select_fusion
  300.5 8.5 %all-to-all-start.1 = ((bf16[16,1,8,128,128]{4,3,2,1,0:T(8,128)(2,1)}), bf16[16,1,8,128,128]{4,3,2,1,0:T(8,128)(2,1)}, u32[]{:S(2)}, u32[]{:S(2)}) async-start(bf16[16,1,8,128,128]{4,3,2,1,0:T(8,128)(2,1)} %broadcast_select_fusion), calls=%async_computation.2 | async-start | bytes 8388608 | tf_op jit(solution)/shard_map/all_to_all | solution.py:79
  309.0 0.2 reduce-scatter.5.cloned.1.call-start
  309.2 0.3 select_reduce_fusion
  309.8 1.3 gather_fusion.8
  311.3 0.4 fusion.34
  311.8 23.3 %gather_fusion.3 = bf16[1024,128,128]{2,1,0:T(8,128)(2,1)} fusion(bf16[16,8,128,128]{3,2,1,0:T(8,128)(2,1)} %param.11, s32[1024]{0:T(1024)S(1)} %reshape.666), kind=kCustom, calls=%fused_computation.5 | custom fusion | bytes 67117056 | tf_op jit(solution)/shard_map/gather | solution.py:44
  335.1 34.6 %all-to-all-done.1 = bf16[16,1,8,128,128]{4,3,2,1,0:T(8,128)(2,1)} async-done(((bf16[16,1,8,128,128]{4,3,2,1,0:T(8,128)(2,1)}), bf16[16,1,8,128,128]{4,3,2,1,0:T(8,128)(2,1)}, u32[]{:S(2)}, u32[]{:S(2)}) %all-to-all-start.1) | async-done | bytes 4194336 | tf_op jit(solution)/shard_map/all_to_all | solution.py:79
  369.8 17.9 %bitcast_convert_fusion = bf16[16,8,128,128]{3,2,1,0:T(8,128)(2,1)} fusion(bf16[16,8,8,128,128]{4,3,2,1,0:T(8,128)(2,1)} %bitcast.168, bf16[16,1,8,128,128]{4,3,2,1,0:T(8,128)(2,1)} %all-to-all-done.1), kind=kOutput, calls=%fused_computation.9 | convolution fusion | flops 4297064448 | bytes 41943040 | tf_op jit(solution)/shard_map/kabij,kbjl->kail/dot_general | solution.py:45
  387.8 0.6 dynamic_slice.23
  392.6 0.3 fusion.22
  392.9 20.8 %all-gather = bf16[1024,128]{0,1:T(8,128)(2,1)S(1)} all-gather(bf16[128,128]{0,1:T(8,128)(2,1)S(1)} %fusion.22), channel_id=2, replica_groups=mesh['prow'=8,'pcol'=16] {'prow'}, dimensions={0}, use_global_device_ids=true | all-gather | bytes 294912 | tf_op jit(solution)/shard_map/all_gather | solution.py:6
  413.8 0.2 bitcast_reduce_fusion
  414.1 3.0 gather_fusion.5
  417.2 0.9 fusion.21
  418.0 57.1 %reduce-scatter.5.cloned.1.call-done = bf16[1,8,128,128]{3,2,1,0:T(8,128)(2,1)} async-done(((bf16[16,8,128,128]{3,2,1,0:T(8,128)(2,1)}), bf16[1,8,128,128]{3,2,1,0:T(8,128)(2,1)}) %reduce-scatter.5.cloned.1.call-update) | async-done | bytes 262160 | tf_op jit(solution)/shard_map/reduce_scatter | solution.py:81
  475.1 1.2 fusion.10
  476.3 0.9 fusion.20
  477.2 24.7 %all_gather.23 = bf16[16,128,128]{2,1,0:T(8,128)(2,1)S(1)} all-gather(bf16[1,128,128]{2,1,0:T(8,128)(2,1)S(1)} %copy.199), channel_id=1, replica_groups=mesh['prow'=8,'pcol'=16] {'pcol'}, dimensions={0}, use_global_device_ids=true | all-gather | bytes 557056 | tf_op jit(solution)/shard_map/all_gather | solution.py:96
  501.9 44.9 %all-reduce.6.cloned.1.call-done = (bf16[1,128,128]{2,1,0:T(8,128)(2,1)}, bf16[1,128,128]{1,2,0:T(8,128)(2,1)}) async-done(((bf16[1,128,128]{2,1,0:T(8,128)(2,1)}, bf16[1,128,128]{1,2,0:T(8,128)(2,1)}), (bf16[1,128,128]{2,1,0:T(8,128)(2,1)}, bf16[1,128,128]{1,2,0:T(8,128)(2,1)})) %all-reduce.6.cloned.1.call-update) | async-done | bytes 65552 | tf_op jit(solution)/shard_map/psum | solution.py:113
  546.8 0.9 fusion.16
  547.7 1.0 fusion.15
  548.7 0.7 copy.200
  (87 shorter events, 2.9 us)
Async XLA Ops:
  7.2 468.0 %copy-start = (bf16[1,128,128]{2,1,0:T(8,128)(2,1)S(1)}, bf16[1,128,128]{2,1,0:T(8,128)(2,1)}, u32[]{:S(2)}) copy-start(bf16[1,128,128]{2,1,0:T(8,128)(2,1)} %param.18) | copy-start | bytes 98308
  7.2 55.4 %all-gather.5.cloned.1.call-start = ((), (), s32[]{:S(2)}) async-start(), calls=%async_computation.4 | async-start | bytes 2359296 | tf_op jit(solution)/shard_map/all_gather | solution.py:67
  71.8 8.7 %copy-start.11 = (s32[16]{0:T(128)S(1)}, s32[16]{0:T(128)}, u32[]{:S(2)}) copy-start(s32[16]{0:T(128)} %param.15) | copy-start | bytes 196
  71.8 8.7 %copy-start.1 = (s32[16,64]{1,0:T(8,128)S(1)}, s32[16,64]{1,0:T(8,128)}, u32[]{:S(2)}) copy-start(s32[16,64]{1,0:T(8,128)} %param.12) | copy-start | bytes 12292
  71.8 9.3 %copy-start.10 = (s32[16,64]{1,0:T(8,128)S(1)}, s32[16,64]{1,0:T(8,128)}, u32[]{:S(2)}) copy-start(s32[16,64]{1,0:T(8,128)} %param.16) | copy-start | bytes 12292
  71.8 64.0 %all-to-all-start = ((bf16[16,1,8,128,128]{4,3,2,1,0:T(8,128)(2,1)}), bf16[16,1,8,128,128]{4,3,2,1,0:T(8,128)(2,1)}, u32[]{:S(2)}, u32[]{:S(2)}) async-start(bf16[16,1,8,128,128]{4,3,2,1,0:T(8,128)(2,1)} %broadcast_select_fusion.1), calls=%async_computation | async-start | bytes 8388608 | tf_op jit(solution)/shard_map/all_to_all | solution.py:69
  80.4 159.4 %reduce-scatter.3.cloned.1.call-start = ((), (), s32[]{:S(2)}) async-start(), calls=%async_computation.5 | async-start | bytes 4456448 | tf_op jit(solution)/shard_map/reduce_scatter | solution.py:71
  153.5 137.9 %all-gather.7.cloned.1.call-start = ((), (), s32[]{:S(2)}) async-start(), calls=%async_computation.6 | async-start | bytes 2359296 | tf_op jit(solution)/shard_map/all_gather | solution.py:77
  154.2 259.9 %all-gather.9.cloned.1.call-start = ((), (), s32[]{:S(2)}) async-start(), calls=%async_computation.8 | async-start | bytes 4456448 | tf_op jit(solution)/shard_map/all_gather | solution.py:95
  300.5 69.3 %all-to-all-start.1 = ((bf16[16,1,8,128,128]{4,3,2,1,0:T(8,128)(2,1)}), bf16[16,1,8,128,128]{4,3,2,1,0:T(8,128)(2,1)}, u32[]{:S(2)}, u32[]{:S(2)}) async-start(bf16[16,1,8,128,128]{4,3,2,1,0:T(8,128)(2,1)} %broadcast_select_fusion), calls=%async_computation.2 | async-start | bytes 8388608 | tf_op jit(solution)/shard_map/all_to_all | solution.py:79
  309.0 166.2 %reduce-scatter.5.cloned.1.call-start = ((), (), s32[]{:S(2)}) async-start(), calls=%async_computation.7 | async-start | bytes 4456448 | tf_op jit(solution)/shard_map/reduce_scatter | solution.py:81
  387.7 2.0 copy-start.8
  387.7 3.4 copy-start.9
  387.7 4.9 copy-start.3
  387.7 4.9 copy-start.5
  387.7 29.5 %copy-start.2 = (bf16[1,8,128,128]{3,2,1,0:T(8,128)(2,1)S(1)}, bf16[1,8,128,128]{3,2,1,0:T(8,128)(2,1)}, u32[]{:S(2)}) copy-start(bf16[1,8,128,128]{3,2,1,0:T(8,128)(2,1)} %param.17) | copy-start | bytes 786436
  387.7 159.1 %all-reduce.6.cloned.1.call-start = ((), (), s32[]{:S(2)}) async-start(), calls=%async_computation.9 | async-start | bytes 131072 | tf_op jit(solution)/shard_map/psum | solution.py:113
  414.1 135.3 %copy-start.6 = (bf16[1,128,128]{2,1,0:T(8,128)(2,1)}, bf16[1,128,128]{2,1,0:T(8,128)(2,1)S(1)}, u32[]{:S(2)}) copy-start(bf16[1,128,128]{2,1,0:T(8,128)(2,1)S(1)} %copy.199) | copy-start | bytes 98308
  476.3 73.1 %copy-start.4 = (bf16[1,8,128,128]{3,2,1,0:T(8,128)(2,1)}, bf16[1,8,128,128]{3,2,1,0:T(8,128)(2,1)S(1)}, u32[]{:S(2)}) copy-start(bf16[1,8,128,128]{3,2,1,0:T(8,128)(2,1)S(1)} %fusion.10) | copy-start | bytes 786436
  547.7 1.7 copy-start.7
Sparse Core Ops, SparseCore 0:
  9.6 52.8 all-gather.4
  153.6 86.1 reduce-scatter.2
  241.4 49.8 all-gather.6
  294.2 92.8 all-gather.8
  391.0 84.0 reduce-scatter.4
  478.1 68.7 all-reduce.5
